TPU v7x, 32 devices: a whole 2x2x4 slice. The times are simulated.
32 devices in a mesh: row: 4 (over z), col: 8 (over y, x, core).
Axes of the slice: x: 2, y: 2, z: 4, core: 2. Of those that a mesh axis runs over, the one named last changes fastest.
Arguments:
- spectra: bfloat16 [1024, 32, 128], P(('row', 'col')), may hold values from -6 to 6
- pair_bins: int32 [1024, 1024], P('row', 'col'), may hold values from 0 to 255
- row_subs: int32 [4, 16], P('row'), may hold values from 0 to 31, as said below
- station_subs: int32 [1024, 8], replicated, may hold values from 0 to 31, as said below
- kernel: bfloat16 [32, 256, 256], replicated, may hold values from -0.375 to 0.375
Outputs:
- spectrum: float32 [32, 32, 256], P(('row', 'col'))
Inputs may be any that keep to these rules, and one draw needn't show every extreme that they name: `row_subs`: each row lists 16 distinct subarrays; each subarray is listed for exactly two row blocks. `station_subs`: each station names 8 distinct subarrays, all listed in row_subs for the station's row block.
All inputs are finite; a program needn't handle non-finite values.
Results may differ from a plain program's by a relative error of at most 0.0039.
Values may be sent and summed in bfloat16 or wider, within the bound.
A program may use at most 64 MiB of HBM per device.

v0:
```python
import math
import jax
import jax.numpy as jnp
from jax import lax
from jax.sharding import PartitionSpec as P

F = 32
NBIN = 256
SUB_DEV = 1


def spread_rows(slot_terms, slot_subs, row_count):
    targets = jnp.arange(row_count, dtype=jnp.int32)
    selector = (targets[:, None] == slot_subs[None, :]).astype(jnp.float32)
    return jnp.dot(selector, slot_terms, precision=lax.Precision.HIGHEST)


def project(owned_bins, kernel):
    velocity_power = jnp.einsum(
        "sfb,fbv->sfv", owned_bins, kernel, preferred_element_type=jnp.float32
    )
    scale = lax.rsqrt(jnp.mean(velocity_power * velocity_power, axis=2, keepdims=True) + 1e-06)
    return velocity_power * scale


def on_device(spectra, pair_bins, row_subs, station_subs, kernel):
    shard_rows = spectra.shape[0]
    col_total = lax.axis_size("col")
    row_index = lax.axis_index("row")
    col_index = lax.axis_index("col")
    row_spectra = lax.all_gather(spectra, "col", axis=0, tiled=True)
    col_spectra = lax.all_gather(spectra, "row", axis=0, tiled=True)
    row_span = row_spectra.shape[0]
    col_span = col_spectra.shape[0]
    slot_subs = row_subs[0]
    slot_count = slot_subs.shape[0]
    row_members = lax.dynamic_slice_in_dim(station_subs, row_index * row_span, row_span, 0)
    positions = jnp.arange(col_span, dtype=jnp.int32)
    col_ids = (
        positions // shard_rows * col_total + col_index
    ) * shard_rows + positions % shard_rows
    col_members = jnp.take(station_subs, col_ids, axis=0)
    row_mask = jnp.any(row_members[None, :, :] == slot_subs[:, None, None], axis=2).astype(
        jnp.bfloat16
    )
    col_mask = jnp.any(col_members[None, :, :] == slot_subs[:, None, None], axis=2).astype(
        jnp.bfloat16
    )
    cross_spec = jnp.einsum(
        "aft,jft->faj", row_spectra, col_spectra, preferred_element_type=jnp.float32
    ).astype(jnp.bfloat16)
    step_rows = math.gcd(row_span, max(1, 2048 // col_span))
    step_count = row_span // step_rows
    bin_ids = jnp.arange(NBIN, dtype=jnp.int32)

    def accumulate(step_index, running):
        first_row = step_index * step_rows
        cross_part = lax.dynamic_slice_in_dim(cross_spec, first_row, step_rows, 1)
        mask_part = lax.dynamic_slice_in_dim(row_mask, first_row, step_rows, 1)
        bins_part = lax.dynamic_slice_in_dim(pair_bins, first_row, step_rows, 0)
        weighted = mask_part[:, None, :, None] * col_mask[:, None, None, :] * cross_part[None]
        onehot = (bins_part.reshape(-1, 1) == bin_ids[None, :]).astype(jnp.bfloat16)
        return running + jnp.dot(
            weighted.reshape(slot_count * F, step_rows * col_span),
            onehot,
            preferred_element_type=jnp.float32,
        )

    partial_value = lax.fori_loop(
        0, step_count, accumulate, jnp.zeros((slot_count * F, NBIN), jnp.float32)
    )
    partial_value = partial_value.reshape(slot_count, F, NBIN)
    freq_part = lax.psum_scatter(partial_value, "col", scatter_dimension=1, tiled=True)
    freq_share = freq_part.shape[1]
    group_rows = SUB_DEV * col_total
    summed = lax.psum_scatter(
        spread_rows(
            freq_part.reshape(slot_count, freq_share * NBIN),
            slot_subs,
            lax.axis_size("row") * group_rows,
        ),
        "row",
        scatter_dimension=0,
        tiled=True,
    )
    binned = summed.reshape(group_rows, freq_share, NBIN).astype(jnp.bfloat16)
    return project(lax.all_to_all(binned, "col", split_axis=0, concat_axis=1, tiled=True), kernel)


def solution(mesh):
    in_specs = (P(("row", "col"), None, None), P("row", "col"), P("row", None), P(), P())
    out_specs = P(("row", "col"), None, None)
    return jax.shard_map(
        on_device, mesh=mesh, in_specs=in_specs, out_specs=out_specs, check_vma=False
    )
```

profile of v0, /device:TPU:0, one launch (start us, length us, event | category | flops | bytes accessed | tf_op | source)
XLA Modules:
  0.0 180.9 jit_solution(14719300169441912463)
XLA Ops:
  6.5 1.8 copy.29
  12.6 27.1 %all-gather.5.cloned.1.call-done = bf16[128,32,128]{2,0,1:T(8,128)(2,1)} async-done(((bf16[32,32,128]{2,0,1:T(8,128)(2,1)}), bf16[128,32,128]{2,0,1:T(8,128)(2,1)}) %all-gather.5.cloned.1.call-update) | async-done | bytes 1048592 | tf_op jit(solution)/shard_map/all_gather | solution.py:32
  39.6 29.4 %all-gather.3.cloned.1.call-done = bf16[256,32,128]{2,0,1:T(8,128)(2,1)} async-done(((bf16[32,32,128]{2,0,1:T(8,128)(2,1)}), bf16[256,32,128]{2,0,1:T(8,128)(2,1)}) %all-gather.3.cloned.1.call-update) | async-done | bytes 2097168 | tf_op jit(solution)/shard_map/all_gather | solution.py:31
  69.0 2.6 %convolution_convert_fusion = bf16[32,256,128]{2,1,0:T(8,128)(2,1)S(1)} fusion(bf16[256,32,128]{2,0,1:T(8,128)(2,1)} %all-gather.3.cloned.1.call-done, bf16[128,32,128]{2,0,1:T(8,128)(2,1)} %all-gather.5.cloned.1.call-done), kind=kOutput, calls=%fused_computation.13 | convolution fusion | flops 269484032 | bytes 5242880 | tf_op jit(solution)/shard_map/aft,jft->faj/dot_general | solution.py:49
  71.6 33.1 %while.14 = (s32[]{:T(128)}, f32[512,256]{1,0:T(8,128)S(1)}, bf16[16,256]{1,0:T(8,128)(2,1)S(1)}, bf16[16,128]{1,0:T(8,128)(2,1)S(1)}, bf16[32,256,128]{2,1,0:T(...) while((s32[]{:T(128)}, f32[512,256]{1,0:T(8,128)S(1)}, ...), condition=%wide.region_3.4_spmd.clone, body=%wide.region_2.3_spmd.clone.sunk | while | flops 538738688 | bytes 5797553 | solution.py:69
  72.7 1.0 fusion.31
  74.8 1.0 fusion.31
  76.8 1.0 fusion.31
  78.9 1.0 fusion.31
  81.0 1.0 fusion.31
  83.0 1.0 fusion.31
  85.1 1.0 fusion.31
  87.2 1.0 fusion.31
  89.3 1.0 fusion.31
  93.4 1.0 fusion.31
  95.5 1.0 fusion.31
  99.6 1.0 fusion.31
  101.7 1.0 fusion.31
  103.8 1.0 fusion.31
  104.8 1.1 copy.31
  105.9 34.2 %reduce-scatter.3.cloned.1.call-done = f32[16,4,256]{2,0,1:T(8,128)} async-done(((f32[16,32,256]{2,0,1:T(8,128)}), f32[16,4,256]{2,0,1:T(8,128)}) %reduce-scatter.3.cloned.1.call-update) | async-done | bytes 65552 | tf_op jit(solution)/shard_map/reduce_scatter | solution.py:73
  141.9 19.9 %reduce-scatter.5.cloned.1.call-done = f32[8,1024]{1,0:T(8,128)} async-done(((f32[32,1024]{1,0:T(8,128)}), f32[8,1024]{1,0:T(8,128)}) %reduce-scatter.5.cloned.1.call-update) | async-done | bytes 32784 | tf_op jit(solution)/shard_map/reduce_scatter | solution.py:76
  162.5 8.2 %all_to_all.4 = bf16[8,4,256]{2,1,0:T(4,128)(2,1)S(1)} all-to-all(bf16[8,4,256]{2,1,0:T(4,128)(2,1)S(1)} %copy.33), channel_id=1, replica_groups=mesh['row'=4,'col'=8] {'col'}, dimensions={0} | all-to-all | bytes 32768 | tf_op jit(solution)/shard_map/all_to_all | solution.py:87
  170.7 2.8 %fusion.22 = f32[32,1,256]{2,1,0:T(1,128)S(1)} fusion(bf16[32,256,1]{1,2,0:T(2,128)(2,1)S(1)} %reshape.159, bf16[32,256,256]{2,1,0:T(8,128)(2,1)} %param.11), kind=kOutput, calls=%fused_computation.49 | convolution fusion | flops 4194304 | bytes 4243456 | tf_op jit(solution)/shard_map/sfb,fbv->sfv/dot_general | solution.py:19
  (113 shorter events, 26.2 us)
Async XLA Ops:
  6.5 5.9 %copy-start = (s32[1,16]{1,0:T(1,128)S(1)}, s32[1,16]{1,0:T(1,128)}, u32[]{:S(2)}) copy-start(s32[1,16]{1,0:T(1,128)} %param.9) | copy-start | bytes 196
  6.5 33.1 %all-gather.5.cloned.1.call-start = ((), (), s32[]{:S(2)}) async-start(), calls=%async_computation.4 | async-start | bytes 1310720 | tf_op jit(solution)/shard_map/all_gather | solution.py:32
  8.3 60.7 %all-gather.3.cloned.1.call-start = ((), (), s32[]{:S(2)}) async-start(), calls=%async_computation.3 | async-start | bytes 2359296 | tf_op jit(solution)/shard_map/all_gather | solution.py:31
  9.1 131.1 %reduce-scatter.3.cloned.1.call-start = ((), (), s32[]{:S(2)}) async-start(), calls=%async_computation.5 | async-start | bytes 589824 | tf_op jit(solution)/shard_map/reduce_scatter | solution.py:73
  105.9 55.8 %reduce-scatter.5.cloned.1.call-start = ((), (), s32[]{:S(2)}) async-start(), calls=%async_computation.6 | async-start | bytes 163840 | tf_op jit(solution)/shard_map/reduce_scatter | solution.py:76
Sparse Core Ops, SparseCore 0:
  8.9 30.6 all-gather.4
  41.5 27.4 all-gather.2
  106.0 34.1 reduce-scatter.2
  142.3 19.4 reduce-scatter.4
where the time goes:
time: 182 us; the launch traced here: 181 us
  waiting for transfers between devices  111 us (61%)
  matrix products  21.9 us (12%)
  local copies, waits for them, and re-layouts  19 us (10%)
  between operations  13.2 us (7%)
  blocking collectives  8.21 us (5%)
  other arithmetic  6.36 us (3%)
    reduce_scatter x1, waiting for transfers between devices, on_device(): lax.psum_scatter(partial_value, 'col', scatter_dimension=1, tiled=True)  34.2 us
    all_gather x1, waiting for transfers between devices, on_device(): row_spectra = lax.all_gather(spectra, 'col', axis=0, tiled=True)  29.4 us
    all_gather x1, waiting for transfers between devices, on_device(): col_spectra = lax.all_gather(spectra, 'row', axis=0, tiled=True)  27.1 us
    reduce_scatter x1, waiting for transfers between devices, on_device(): lax.psum_scatter(spread_rows(freq_part.reshape(slot_count, freq_share * N...  19.9 us
    dot_general x16, matrix products, accumulate(): jnp.dot(weighted.reshape(slot_count * F, step_rows * col_span), onehot, p...  15.6 us
    eq x16, local copies, waits for them, and re-layouts, accumulate(): onehot = (bins_part.reshape(-1, 1) == bin_ids[None, :]).astype(jnp.bfloat16)  11.2 us
    all_to_all x1, blocking collectives, on_device(): lax.all_to_all(binned, 'col', split_axis=0, concat_axis=1, tiled=True)  8.21 us
    mul x32, other arithmetic, accumulate(): mask_part[:, None, :, None] * col_mask[:, None, None, :] * cross_part[None]  3.76 us
  transfers between devices with their start and end apart: 4, of which 4 were waited for; matrix products, arithmetic and copies ran while one was open for 2% of the time, Pallas kernels for 0%

commit v1 on v0

--- a/solution.py
+++ b/solution.py
@@ -29,7 +29,14 @@
     row_index = lax.axis_index("row")
     col_index = lax.axis_index("col")
     row_spectra = lax.all_gather(spectra, "col", axis=0, tiled=True)
-    col_spectra = lax.all_gather(spectra, "row", axis=0, tiled=True)
+    ways, here, step = (lax.axis_size("row"), lax.axis_index("row"), spectra.shape[0])
+    line, have = (spectra, 1)
+    while have < ways:
+        line = jnp.concatenate(
+            [line, lax.ppermute(line, "row", [(d, (d - have) % ways) for d in range(ways)])], axis=0
+        )
+        have = 2 * have
+    col_spectra = jnp.roll(line, here * step, axis=0)
     row_span = row_spectra.shape[0]
     col_span = col_spectra.shape[0]
     slot_subs = row_subs[0]

time: 182 us -> 179 us (0.984)
  waiting for transfers between devices: 111 us -> 80.4 us
  local copies, waits for them, and re-layouts: 19 us -> 38 us
  starting transfers between devices: 0.12 us -> 6.58 us
  other arithmetic: 6.36 us -> 8.23 us
    all_gather x1, waiting for transfers between devices: 29.4 us -> 0.01 us  [on_device(): row_spectra = lax.all_gather(spectra, 'col', axis=0, tiled=True)]
    all_gather x1 -> x0, waiting for transfers between devices: 27.1 us -> none  [on_device(): col_spectra = lax.all_gather(spectra, 'row', axis=0, tiled=True)]
    ppermute x0 -> x2, waiting for transfers between devices: none -> 26.2 us  [on_device(): lax.ppermute(line, 'row', [(d, (d - have) % ways) for d in range(ways)])]
    dynamic_slice x16, local copies, waits for them, and re-layouts: 0.43 us -> 14.9 us  [accumulate(): cross_part = lax.dynamic_slice_in_dim(cross_spec, first_row, step_rows, 1)]
    ppermute x0 -> x2, starting transfers between devices: none -> 6.49 us  [on_device(): lax.ppermute(line, 'row', [(d, (d - have) % ways) for d in range(ways)])]
    unnamed x4 -> x15, local copies, waits for them, and re-layouts: 2.74 us -> 7.2 us
  transfers between devices with their start and end apart: 4 -> 5, of which waited for: 4 -> 4; matrix products, arithmetic and copies ran while one was open for 2% -> 3% of each run, Pallas kernels for 0% -> 0%
where the time goes in v1:
time: 179 us; the launch traced here: 177 us
  waiting for transfers between devices  80.4 us (45%)
  local copies, waits for them, and re-layouts  38 us (21%)
  matrix products  21.9 us (12%)
  between operations  13.3 us (7%)
  other arithmetic  8.23 us (5%)
  blocking collectives  8.2 us (5%)
  starting transfers between devices  6.58 us (4%)
    reduce_scatter x1, waiting for transfers between devices, on_device(): lax.psum_scatter(partial_value, 'col', scatter_dimension=1, tiled=True)  34.1 us
    ppermute x2, waiting for transfers between devices, on_device(): lax.ppermute(line, 'row', [(d, (d - have) % ways) for d in range(ways)])  26.2 us
    reduce_scatter x1, waiting for transfers between devices, on_device(): lax.psum_scatter(spread_rows(freq_part.reshape(slot_count, freq_share * N...  20 us
    dot_general x16, matrix products, accumulate(): jnp.dot(weighted.reshape(slot_count * F, step_rows * col_span), onehot, p...  15.6 us
    dynamic_slice x16, local copies, waits for them, and re-layouts, accumulate(): cross_part = lax.dynamic_slice_in_dim(cross_spec, first_row, step_rows, 1)  14.9 us
    eq x16, local copies, waits for them, and re-layouts, accumulate(): onehot = (bins_part.reshape(-1, 1) == bin_ids[None, :]).astype(jnp.bfloat16)  11.3 us
    all_to_all x1, blocking collectives, on_device(): lax.all_to_all(binned, 'col', split_axis=0, concat_axis=1, tiled=True)  8.2 us
    unnamed x15, local copies, waits for them, and re-layouts  7.2 us
  transfers between devices with their start and end apart: 5, of which 4 were waited for; matrix products, arithmetic and copies ran while one was open for 3% of the time, Pallas kernels for 0%

profile of v1, /device:TPU:0, one launch (start us, length us, event | category | flops | bytes accessed | tf_op | source)
XLA Modules:
  0.0 177.3 jit_solution(8464911716811761680)
XLA Ops:
  6.5 1.8 %constant_dynamic-update-slice_fusion.5 = (bf16[256,32,128]{2,0,1:T(8,128)(2,1)S(1)}, bf16[32,32,128]{2,0,1:T(8,128)(2,1)}) fusion(bf16[32,32,128]{2,1,0:T(8,128)(2,1)} %param.7), kind=kLoop, calls=%fused_computation.30 | loop fusion | bytes 786432
  8.4 5.1 %collective-permute-start = (bf16[32,32,128]{2,0,1:T(8,128)(2,1)}, bf16[32,32,128]{2,0,1:T(8,128)(2,1)S(1)}, u32[]{:S(2)}, u32[]{:S(2)}) collective-permute-start(bf16[32,32,128]{2,0,1:T(8,128)(2,1)} %get-tuple-element.196), channel_id=1, source_target_pairs={{0,24},{8,0},{16,8},{24,16},{1,25},{9,1},{17,9},{25,17},{2,26},{10... | collective-permute-start | bytes 786440 | tf_op jit(solution)/shard_map/ppermute | solution.py:36
  16.7 2.7 %collective-permute-done = bf16[32,32,128]{2,0,1:T(8,128)(2,1)S(1)} collective-permute-done((bf16[32,32,128]{2,0,1:T(8,128)(2,1)}, bf16[32,32,128]{2,0,1:T(8,128)(2,1)S(1)}, u32[]{:S(2)}, u32[]{:S(2)}) %collective-permute-start) | collective-permute-done | bytes 262176 | tf_op jit(solution)/shard_map/ppermute | solution.py:36
  19.4 1.8 %pad_maximum_fusion = bf16[64,32,128]{2,0,1:T(8,128)(2,1)} fusion(bf16[32,32,128]{2,0,1:T(8,128)(2,1)S(1)} %collective-permute-done, bf16[32,32,128]{2,0,1:T(8,128)(2,1)} %get-tuple-element.196), kind=kLoop, calls=%fused_computation.15 | loop fusion | flops 1048576 | bytes 1048576 | tf_op jit(solution)/shard_map/concatenate | solution.py:35
  21.2 1.4 collective-permute-start.1
  23.0 23.4 %collective-permute-done.1 = bf16[64,32,128]{2,0,1:T(8,128)(2,1)S(1)} collective-permute-done((bf16[64,32,128]{2,0,1:T(8,128)(2,1)}, bf16[64,32,128]{2,0,1:T(8,128)(2,1)S(1)}, u32[]{:S(2)}, u32[]{:S(2)}) %collective-permute-start.1) | collective-permute-done | bytes 524320 | tf_op jit(solution)/shard_map/ppermute | solution.py:36
  46.7 1.3 copy-done.1
  48.0 2.6 %convert_bitcast_fusion = bf16[32,256,128]{1,2,0:T(8,128)(2,1)S(1)} fusion(bf16[256,32,128]{2,0,1:T(8,128)(2,1)} %all-gather.2.cloned.1.call-done, bf16[256,32,128]{2,0,1:T(8,128)(2,1)} %copy-done.1, s32[]{:T(128)S(6)} %select_n.90), kind=kOutput, calls=%fused_computation.13 | convolution fusion | flops 269484032 | bytes 5242884 | tf_op jit(solution)/shard_map/aft,jft->faj/dot_general | solution.py:56
  50.7 2.9 %copy.50 = bf16[32,256,128]{2,1,0:T(8,128)(2,1)} copy(bf16[32,256,128]{1,2,0:T(8,128)(2,1)S(1)} %convert_bitcast_fusion) | data formatting | bytes 4194304
  53.6 47.6 %while.14 = (s32[]{:T(128)}, f32[512,256]{1,0:T(8,128)S(1)}, bf16[16,256]{1,0:T(8,128)(2,1)S(1)}, bf16[16,128]{1,0:T(8,128)(2,1)S(1)}, bf16[32,256,128]{2,1,0:T(...) while((s32[]{:T(128)}, f32[512,256]{1,0:T(8,128)S(1)}, ...), condition=%wide.region_3.4_spmd.clone, body=%wide.region_2.3_spmd.clone.sunk | while | flops 538738688 | bytes 5797545 | solution.py:76
  55.5 1.0 fusion.32
  58.5 1.0 fusion.32
  61.5 1.0 fusion.32
  64.5 1.0 fusion.32
  67.4 1.0 fusion.32
  70.4 1.0 fusion.32
  73.4 1.0 fusion.32
  88.3 1.0 fusion.32
  100.1 1.0 fusion.32
  101.1 1.1 copy.51
  102.3 34.1 %reduce-scatter.3.cloned.1.call-done = f32[16,4,256]{2,0,1:T(8,128)} async-done(((f32[16,32,256]{2,0,1:T(8,128)}), f32[16,4,256]{2,0,1:T(8,128)}) %reduce-scatter.3.cloned.1.call-update) | async-done | bytes 65552 | tf_op jit(solution)/shard_map/reduce_scatter | solution.py:80
  138.1 20.0 %reduce-scatter.5.cloned.1.call-done = f32[8,1024]{1,0:T(8,128)} async-done(((f32[32,1024]{1,0:T(8,128)}), f32[8,1024]{1,0:T(8,128)}) %reduce-scatter.5.cloned.1.call-update) | async-done | bytes 32784 | tf_op jit(solution)/shard_map/reduce_scatter | solution.py:83
  158.9 8.2 %all_to_all.4 = bf16[8,4,256]{2,1,0:T(4,128)(2,1)S(1)} all-to-all(bf16[8,4,256]{2,1,0:T(4,128)(2,1)S(1)} %copy.53), channel_id=1, replica_groups=mesh['row'=4,'col'=8] {'col'}, dimensions={0} | all-to-all | bytes 32768 | tf_op jit(solution)/shard_map/all_to_all | solution.py:94
  167.1 2.8 %fusion.24 = f32[32,1,256]{2,1,0:T(1,128)S(1)} fusion(bf16[32,256,1]{1,2,0:T(2,128)(2,1)S(1)} %reshape.159, bf16[32,256,256]{2,1,0:T(8,128)(2,1)} %param.11), kind=kOutput, calls=%fused_computation.58 | convolution fusion | flops 4194304 | bytes 4243456 | tf_op jit(solution)/shard_map/sfb,fbv->sfv/dot_general | solution.py:19
  (127 shorter events, 45.2 us)
Async XLA Ops:
  6.5 16.2 %copy-start.3 = (s32[1,16]{1,0:T(1,128)S(1)}, s32[1,16]{1,0:T(1,128)}, u32[]{:S(2)}) copy-start(s32[1,16]{1,0:T(1,128)} %param.9) | copy-start | bytes 196
  6.5 41.5 %all-gather.2.cloned.1.call-start = ((), (), s32[]{:S(2)}) async-start(), calls=%async_computation.3 | async-start | bytes 2359296 | tf_op jit(solution)/shard_map/all_gather | solution.py:31
  8.4 38.1 %copy-start = (bf16[32,32,128]{2,1,0:T(8,128)(2,1)S(1)}, bf16[32,32,128]{2,1,0:T(8,128)(2,1)}, u32[]{:S(2)}) copy-start(bf16[32,32,128]{2,1,0:T(8,128)(2,1)} %param.7) | copy-start | bytes 786436
  8.4 128.1 %reduce-scatter.3.cloned.1.call-start = ((), (), s32[]{:S(2)}) async-start(), calls=%async_computation.4 | async-start | bytes 589824 | tf_op jit(solution)/shard_map/reduce_scatter | solution.py:80
  8.4 11.0 %collective-permute-start = (bf16[32,32,128]{2,0,1:T(8,128)(2,1)}, bf16[32,32,128]{2,0,1:T(8,128)(2,1)S(1)}, u32[]{:S(2)}, u32[]{:S(2)}) collective-permute-start(bf16[32,32,128]{2,0,1:T(8,128)(2,1)} %get-tuple-element.196), channel_id=1, source_target_pairs={{0,24},{8,0},{16,8},{24,16},{1,25},{9,1},{17,9},{25,17},{2,26},{10... | collective-permute-start | bytes 786440 | tf_op jit(solution)/shard_map/ppermute | solution.py:36
  21.2 25.2 %collective-permute-start.1 = (bf16[64,32,128]{2,0,1:T(8,128)(2,1)}, bf16[64,32,128]{2,0,1:T(8,128)(2,1)S(1)}, u32[]{:S(2)}, u32[]{:S(2)}) collective-permute-start(bf16[64,32,128]{2,0,1:T(8,128)(2,1)} %pad_maximum_fusion), channel_id=1, source_target_pairs={{0,16},{8,24},{16,0},{24,8},{1,17},{9,25},{17,1},{25,9},{2,18},{10... | collective-permute-start | bytes 1572872 | tf_op jit(solution)/shard_map/ppermute | solution.py:36
  46.7 1.3 copy-start.1
  50.7 2.9 %copy-start.2 = (f32[512,256]{1,0:T(8,128)S(1)}, f32[512,256]{1,0:T(8,128)}, u32[]{:S(2)}) copy-start(f32[512,256]{1,0:T(8,128)} %custom-call) | copy-start | bytes 1572868
  102.3 55.9 %reduce-scatter.5.cloned.1.call-start = ((), (), s32[]{:S(2)}) async-start(), calls=%async_computation.5 | async-start | bytes 163840 | tf_op jit(solution)/shard_map/reduce_scatter | solution.py:83
Sparse Core Ops, SparseCore 0:
  9.2 30.8 all-gather.1
  102.4 34.0 reduce-scatter.2
  138.7 19.4 reduce-scatter.4
